TPU v7x, 32 devices: a whole 2x2x4 slice. The times are simulated.
32 devices in a mesh: shot: 8 (over y, x, core), rcv: 4 (over z).
Axes of the slice: x: 2, y: 2, z: 4, core: 2. Of those that a mesh axis runs over, the one named last changes fastest.
Arguments:
- traces: bfloat16 [256, 512, 256], P('shot', 'rcv'), may hold values from -6 to 6
- shift_index: int32 [256, 512], P('shot', 'rcv'), may hold values from 0 to 63
- deconv: float32 [256, 64], P('shot'), may hold values from -0.75 to 0.75
- focal_start: bfloat16 [8, 512, 256], P(None, 'rcv'), may hold values from -6 to 6
- onset_source: int32 [8, 256], P('rcv', 'shot'), may hold values from 32 to 128
- onset_receiver: int32 [8, 512], P('shot', 'rcv'), may hold values from 32 to 128
Outputs:
- upgoing_first: float32 [8, 256, 256], P('rcv', 'shot')
- downgoing: float32 [8, 512, 256], P('shot', 'rcv')
- upgoing_second: float32 [8, 256, 256], P('rcv', 'shot')
All inputs are finite; a program needn't handle non-finite values.
Results may differ from a plain program's by a relative error of at most 0.028.
Values may be sent and summed in bfloat16 or wider, within the bound.
No kernel may reach another device: no remote copies, remote signals or barrier semaphores. Data moves between devices by JAX's collectives and lax.ppermute only.
A program may use at most 64 MiB of HBM per device.

v0:
```python
import math
import jax
import jax.numpy as jnp
from jax import lax
from jax.sharding import PartitionSpec as P

NT = 256
NF = 128
TAPS = 64
KSHIFT = 64
exact_mode = lax.Precision.HIGHEST


def fourier_tables(length, bin_count):
    sample_ids = jnp.arange(length, dtype=jnp.int32)
    bin_ids = jnp.arange(bin_count, dtype=jnp.int32)
    phases = sample_ids[:, None] * bin_ids[None, :] % length
    angles = 2.0 * math.pi / length * phases.astype(jnp.float32)
    forward = jnp.concatenate([jnp.cos(angles), -jnp.sin(angles)], axis=1)
    weights = jnp.where(bin_ids == 0, 1.0, 2.0).astype(jnp.float32) / length
    inverse = jnp.concatenate(
        [jnp.cos(angles) * weights[None, :], -jnp.sin(angles) * weights[None, :]], axis=1
    ).T
    return (forward, inverse)


def delay_table(tap_count, kind_count):
    tap_index = jnp.arange(tap_count, dtype=jnp.float32)
    fraction = jnp.arange(kind_count, dtype=jnp.float32) * (tap_count / (4.0 * kind_count))
    offset = tap_index[None, :] - 0.375 * tap_count - fraction[:, None]
    window = 0.5 - 0.5 * jnp.cos(2.0 * math.pi * (tap_index + 0.5) / tap_count)
    return jnp.sinc(offset) * window[None, :]


def split_transform(signal, upper_part, lower_part, form):
    high_term = jnp.einsum(form, signal, upper_part, preferred_element_type=jnp.float32)
    low_term = jnp.einsum(form, signal, lower_part, preferred_element_type=jnp.float32)
    return high_term + low_term


def complex_product(left_op, right_op):
    real_part = left_op[0] * right_op[0] - left_op[1] * right_op[1]
    imag_part = left_op[0] * right_op[1] + left_op[1] * right_op[0]
    return jnp.stack([real_part, imag_part])


def apply_forward(matrix, focal_spec):

    def product_term(left_op, right_op):
        return jnp.einsum("fdau,fpd->fapu", left_op, right_op, preferred_element_type=jnp.float32)

    real_part = product_term(matrix[0], focal_spec[0]) - product_term(matrix[1], focal_spec[1])
    imag_part = product_term(matrix[0], focal_spec[1]) + product_term(matrix[1], focal_spec[0])
    return jnp.stack([real_part, imag_part])


def apply_adjoint(matrix, echo_spec):

    def product_term(left_op, right_op):
        return jnp.einsum("fdau,fapu->fpd", left_op, right_op, preferred_element_type=jnp.float32)

    real_part = product_term(matrix[0], echo_spec[0]) + product_term(matrix[1], echo_spec[1])
    imag_part = product_term(matrix[0], echo_spec[1]) - product_term(matrix[1], echo_spec[0])
    stacked = jnp.stack([real_part, imag_part])
    return stacked.reshape(
        stacked.shape[0], stacked.shape[1], stacked.shape[2], 1, stacked.shape[3]
    )


def to_time_field(spectra, onset, inverse):
    flat = spectra.reshape(-1, onset.shape[0], onset.shape[1])
    signal = jnp.einsum("cpu,ct->put", flat, inverse, precision=exact_mode)
    sample_ids = jnp.arange(inverse.shape[1], dtype=jnp.int32)
    folded = jnp.minimum(sample_ids, inverse.shape[1] - sample_ids)
    return jnp.where(folded[None, None, :] < onset[:, :, None], signal, 0.0)


def to_spectrum(signal, forward):
    flat = jnp.einsum("put,tc->cpu", signal, forward, precision=exact_mode)
    return flat.reshape(2, flat.shape[0] // 2, flat.shape[1], flat.shape[2])


def forward_sum(partial_value):
    return lax.psum_scatter(
        partial_value.astype(jnp.bfloat16), "rcv", scatter_dimension=3, tiled=True
    ).astype(jnp.float32)


def focal_rows(pieces):
    return lax.all_gather(pieces, "rcv", axis=3, tiled=True)


def time_layout(spectra):
    return lax.all_to_all(
        spectra.astype(jnp.bfloat16), "shot", split_axis=2, concat_axis=1, tiled=True
    ).astype(spectra.dtype)


def spectrum_layout(spectra):
    return lax.all_to_all(spectra, "shot", split_axis=1, concat_axis=2, tiled=True)


def body(traces, shift_index, deconv, focal_start, onset_source, onset_receiver):
    shot_count = lax.axis_size("shot")
    rcv_count = lax.axis_size("rcv")
    shot_index = lax.axis_index("shot")
    per_owner = NF // shot_count
    source_local = traces.shape[0]
    receiver_local = traces.shape[1]
    focal_total = focal_start.shape[0]
    focal_owned = focal_total // shot_count
    gain_factor = 1.0 / math.sqrt(NT * receiver_local * rcv_count)
    forward, inverse = fourier_tables(NT, NF)
    upper_part = forward.astype(jnp.bfloat16)
    lower_part = (forward - upper_part.astype(jnp.float32)).astype(jnp.bfloat16)
    tap_spec = jnp.dot(delay_table(TAPS, KSHIFT), forward[:TAPS], precision=exact_mode)
    wave_spec = jnp.dot(deconv, forward[:TAPS], precision=exact_mode)
    raw_spec = split_transform(traces, upper_part, lower_part, "srt,tc->crs").reshape(
        2, NF, receiver_local, source_local
    )
    kind_ids = jnp.arange(KSHIFT, dtype=jnp.int32)
    one_hot = (shift_index[:, :, None] == kind_ids[None, None, :]).astype(jnp.float32)
    delays = jnp.einsum("srm,mc->crs", one_hot, tap_spec, precision=exact_mode).reshape(
        2, NF, receiver_local, source_local
    )
    wavelet = wave_spec.T.reshape(2, NF, 1, source_local)
    reflection = (complex_product(complex_product(raw_spec, delays), wavelet) * gain_factor).astype(
        jnp.bfloat16
    )
    owned = lax.all_to_all(reflection, "shot", split_axis=1, concat_axis=3, tiled=True)
    matrix = owned.reshape(2, per_owner, receiver_local, shot_count, source_local)
    upper_band = lax.dynamic_slice_in_dim(
        upper_part.reshape(NT, 2, NF), shot_index * per_owner, per_owner, 2
    ).reshape(NT, 2 * per_owner)
    lower_band = lax.dynamic_slice_in_dim(
        lower_part.reshape(NT, 2, NF), shot_index * per_owner, per_owner, 2
    ).reshape(NT, 2 * per_owner)
    start_spec = split_transform(focal_start, upper_band, lower_band, "prt,tc->cpr").reshape(
        2, per_owner, focal_total, receiver_local
    )
    start_spec = start_spec.astype(jnp.bfloat16)
    summed = forward_sum(apply_forward(matrix, start_spec))
    summed = time_layout(summed)
    upgoing_first = to_time_field(summed, onset_source, inverse)
    echo_spec = to_spectrum(upgoing_first, forward).astype(jnp.bfloat16)
    echo_spec = echo_spec.reshape(2, NF, 1, echo_spec.shape[2], echo_spec.shape[3])
    echo_spec = spectrum_layout(echo_spec)
    echo_all = focal_rows(echo_spec)
    adjoint = apply_adjoint(matrix, echo_all)
    adjoint = time_layout(adjoint)
    focal_own = lax.dynamic_slice_in_dim(
        focal_start, shot_index * focal_owned, focal_owned, 0
    ).astype(jnp.float32)
    downgoing = focal_own + to_time_field(adjoint, onset_receiver, inverse)
    plus_spec = to_spectrum(downgoing, forward).astype(jnp.bfloat16)
    plus_spec = plus_spec.reshape(2, NF, focal_owned, 1, receiver_local)
    plus_spec = spectrum_layout(plus_spec)
    plus_spec = plus_spec.reshape(2, plus_spec.shape[1], focal_total, receiver_local)
    summed_again = forward_sum(apply_forward(matrix, plus_spec))
    summed_again = time_layout(summed_again)
    upgoing_second = to_time_field(summed_again, onset_source, inverse)
    return (upgoing_first, downgoing, upgoing_second)


def solution(mesh):
    placed = (
        P("shot", "rcv", None),
        P("shot", "rcv"),
        P("shot", None),
        P(None, "rcv", None),
        P("rcv", "shot"),
        P("shot", "rcv"),
    )
    return jax.shard_map(
        body,
        mesh=mesh,
        in_specs=placed,
        out_specs=(P("rcv", "shot", None), P("shot", "rcv", None), P("rcv", "shot", None)),
        check_vma=False,
    )
```

profile of v0, /device:TPU:0, one launch (start us, length us, event | category | flops | bytes accessed | tf_op | source)
XLA Modules:
  0.0 180.0 jit_solution(3745824398154742096)
XLA Ops:
  7.8 1.0 copy-done
  10.9 1.8 %convolution_bitcast_fusion = f32[256,128,32]{1,0,2:T(8,128)S(1)} fusion(f32[64,256,1]{1,0,2:T(8,128)S(1)} %convolution_bitcast_fusion.5, s32[32,128]{1,0:T(8,128)S(1)} %copy-done.7), kind=kOutput, calls=%fused_computation.3 | convolution fusion | flops 805568512 | bytes 4276224 | tf_op jit(solution)/shard_map/srm,mc->crs/dot_general | solution.py:123
  12.8 1.5 subtract_bitcast_fusion
  14.3 1.3 add_bitcast_fusion.1
  16.2 2.7 %copy.58 = bf16[2,128,128,32]{2,3,0,1:T(8,128)(2,1)} copy(bf16[2,128,128,32]{2,1,3,0:T(8,128)(2,1)S(1)} %fusion) | data formatting | bytes 4194304 | tf_op jit(solution)/shard_map/convert_element_type | solution.py:127
  18.8 5.3 %all-to-all-start = ((bf16[2,128,128,32]{2,3,0,1:T(8,128)(2,1)}), bf16[2,128,128,32]{2,3,0,1:T(8,128)(2,1)}, u32[]{:S(2)}, u32[]{:S(2)}) async-start(bf16[2,128,128,32]{2,3,0,1:T(8,128)(2,1)} %copy.58), calls=%async_computation | async-start | bytes 4194304 | tf_op jit(solution)/shard_map/all_to_all | solution.py:130
  25.5 25.4 %all-to-all-done = bf16[2,128,128,32]{2,3,0,1:T(8,128)(2,1)} async-done(((bf16[2,128,128,32]{2,3,0,1:T(8,128)(2,1)}), bf16[2,128,128,32]{2,3,0,1:T(8,128)(2,1)}, u32[]{:S(2)}, u32[]{:S(2)}) %all-to-all-start) | async-done | bytes 2097184 | tf_op jit(solution)/shard_map/all_to_all | solution.py:130
  50.9 2.2 %copy.136 = bf16[2,8,16,128,32]{3,4,1,2,0:T(8,128)(2,1)S(1)} copy(bf16[2,8,16,128,32]{3,4,0,2,1:T(8,128)(2,1)} %bitcast.12) | data formatting | bytes 4194304 | tf_op jit(solution)/shard_map/all_to_all | solution.py:130
  53.1 1.4 fusion.23
  54.6 1.5 fusion.22
  56.0 1.5 fusion.8
  57.5 1.5 fusion.7
  59.1 0.9 copy.65
  60.6 21.2 %reduce-scatter.3.cloned.1.call-done = bf16[2,16,8,2,32]{4,2,1,0,3:T(8,128)(2,1)} async-done(((bf16[2,16,8,8,32]{4,2,1,0,3:T(8,128)(2,1)}), bf16[2,16,8,2,32]{4,2,1,0,3:T(8,128)(2,1)}) %reduce-scatter.3.cloned.1.call-update) | async-done | bytes 32784 | tf_op jit(solution)/shard_map/reduce_scatter | solution.py:84
  81.8 1.0 copy.139
  82.8 0.8 reshape.232
  83.6 3.6 %all-to-all-start.1 = ((bf16[8,2,1024]{2,1,0:T(2,128)(2,1)}), bf16[8,2,1024]{2,1,0:T(2,128)(2,1)S(1)}, u32[]{:S(2)}, u32[]{:S(2)}) async-start(bf16[8,2,1024]{2,1,0:T(2,128)(2,1)} %reshape.232), calls=%async_computation.2 | async-start | bytes 65536 | tf_op jit(solution)/shard_map/all_to_all | solution.py:94
  87.2 4.8 %all-to-all-done.1 = bf16[8,2,1024]{2,1,0:T(2,128)(2,1)S(1)} async-done(((bf16[8,2,1024]{2,1,0:T(2,128)(2,1)}), bf16[8,2,1024]{2,1,0:T(2,128)(2,1)S(1)}, u32[]{:S(2)}, u32[]{:S(2)}) %all-to-all-start.1) | async-done | bytes 32800 | tf_op jit(solution)/shard_map/all_to_all | solution.py:94
  93.3 7.2 %all_to_all.93 = bf16[8,2,1024]{2,1,0:T(2,128)(2,1)S(1)} all-to-all(bf16[8,2,1024]{2,1,0:T(2,128)(2,1)S(1)} %reshape.234), channel_id=1, replica_groups=mesh['shot'=8,'rcv'=4] {'shot'}, dimensions={0} | all-to-all | bytes 65536 | tf_op jit(solution)/shard_map/all_to_all | solution.py:100
  100.8 16.1 %all-gather = bf16[2,16,8,1,8,32]{5,2,3,1,0,4:T(8,128)(2,1)S(1)} all-gather(bf16[2,16,8,1,2,32]{5,2,3,1,0,4:T(8,128)(2,1)S(1)} %copy.73), channel_id=2, replica_groups=mesh['shot'=8,'rcv'=4] {'rcv'}, dimensions={4}, use_global_device_ids=true | all-gather | bytes 163840 | tf_op jit(solution)/shard_map/all_gather | solution.py:90
  119.5 3.4 %all-to-all-start.3 = ((bf16[2,16,8,1,128]{4,1,3,0,2:T(8,128)(2,1)}), bf16[2,16,8,1,128]{4,1,3,0,2:T(8,128)(2,1)S(1)}, u32[]{:S(2)}, u32[]{:S(2)}) async-start(bf16[2,16,8,1,128]{4,1,3,0,2:T(8,128)(2,1)} %copy.76), calls=%async_computation.4 | async-start | bytes 131072 | tf_op jit(solution)/shard_map/all_to_all | solution.py:94
  123.0 4.9 %all-to-all-done.3 = bf16[2,16,8,1,128]{4,1,3,0,2:T(8,128)(2,1)S(1)} async-done(((bf16[2,16,8,1,128]{4,1,3,0,2:T(8,128)(2,1)}), bf16[2,16,8,1,128]{4,1,3,0,2:T(8,128)(2,1)S(1)}, u32[]{:S(2)}, u32[]{:S(2)}) %all-to-all-start.3) | async-done | bytes 65568 | tf_op jit(solution)/shard_map/all_to_all | solution.py:94
  128.6 7.4 %all_to_all.94 = bf16[2,128,1,1,128]{4,0,3,2,1:T(2,128)(2,1)S(1)} all-to-all(bf16[2,128,1,1,128]{4,0,3,2,1:T(2,128)(2,1)S(1)} %copy.78), channel_id=1, replica_groups=mesh['shot'=8,'rcv'=4] {'shot'}, dimensions={1} | all-to-all | bytes 131072 | tf_op jit(solution)/shard_map/all_to_all | solution.py:100
  136.1 2.7 %fusion.21 = f32[16,8,8,32]{3,1,2,0:T(8,128)S(1)} fusion(bf16[2,16,128,8,32]{2,4,3,1,0:T(8,128)(2,1)} %bitcast.192, bf16[2,16,8,1,1,128]{5,2,1,4,3,0:T(8,128)(2,1)S(1)} %bitcast.201), kind=kOutput, calls=%fused_computation.49 | convolution fusion | flops 8388608 | bytes 1212416 | tf_op jit(solution)/shard_map/fdau,fpd->fapu/dot_general | solution.py:50
  138.7 1.5 fusion.20
  140.2 1.5 fusion.6
  141.7 1.5 fusion.5
  143.3 0.9 copy.81
  144.2 18.3 %reduce-scatter.5.cloned.1.call-done = bf16[2,16,8,2,32]{4,2,1,0,3:T(8,128)(2,1)} async-done(((bf16[2,16,8,8,32]{4,2,1,0,3:T(8,128)(2,1)}), bf16[2,16,8,2,32]{4,2,1,0,3:T(8,128)(2,1)}) %reduce-scatter.5.cloned.1.call-update) | async-done | bytes 32784 | tf_op jit(solution)/shard_map/reduce_scatter | solution.py:84
  162.5 1.0 copy.138
  163.7 8.3 %all_to_all.95 = bf16[8,2,1024]{2,1,0:T(2,128)(2,1)S(1)} all-to-all(bf16[8,2,1024]{2,1,0:T(2,128)(2,1)S(1)} %reshape.236), channel_id=1, replica_groups=mesh['shot'=8,'rcv'=4] {'shot'}, dimensions={0} | all-to-all | bytes 65536 | tf_op jit(solution)/shard_map/all_to_all | solution.py:94
  172.3 0.9 convolution_select_fusion.1
  (74 shorter events, 10.7 us)
Async XLA Ops:
  7.2 1.6 copy-start
  9.5 0.8 copy-start.8
  9.5 1.4 copy-start.7
  18.8 6.1 %copy-start.4 = (bf16[8,128,256]{2,1,0:T(8,128)(2,1)S(1)}, bf16[8,128,256]{2,1,0:T(8,128)(2,1)}, u32[]{:S(2)}) copy-start(bf16[8,128,256]{2,1,0:T(8,128)(2,1)} %param.9) | copy-start | bytes 1572868
  18.8 32.1 %all-to-all-start = ((bf16[2,128,128,32]{2,3,0,1:T(8,128)(2,1)}), bf16[2,128,128,32]{2,3,0,1:T(8,128)(2,1)}, u32[]{:S(2)}, u32[]{:S(2)}) async-start(bf16[2,128,128,32]{2,3,0,1:T(8,128)(2,1)} %copy.58), calls=%async_computation | async-start | bytes 4194304 | tf_op jit(solution)/shard_map/all_to_all | solution.py:130
  24.1 57.6 %reduce-scatter.3.cloned.1.call-start = ((), (), s32[]{:S(2)}) async-start(), calls=%async_computation.8 | async-start | bytes 655360 | tf_op jit(solution)/shard_map/reduce_scatter | solution.py:84
  53.1 4.4 %copy-start.1 = (bf16[2,8,16,128,32]{3,4,1,2,0:T(8,128)(2,1)}, bf16[2,8,16,128,32]{3,4,1,2,0:T(8,128)(2,1)S(1)}, u32[]{:S(2)}) copy-start(bf16[2,8,16,128,32]{3,4,1,2,0:T(8,128)(2,1)S(1)} %copy.136) | copy-start | bytes 6291460
  59.0 33.4 %copy-start.9 = (s32[2,32]{1,0:T(2,128)S(1)}, s32[2,32]{1,0:T(2,128)}, u32[]{:S(2)}) copy-start(s32[2,32]{1,0:T(2,128)} %param.10) | copy-start | bytes 772
  83.6 8.5 %all-to-all-start.1 = ((bf16[8,2,1024]{2,1,0:T(2,128)(2,1)}), bf16[8,2,1024]{2,1,0:T(2,128)(2,1)S(1)}, u32[]{:S(2)}, u32[]{:S(2)}) async-start(bf16[8,2,1024]{2,1,0:T(2,128)(2,1)} %reshape.232), calls=%async_computation.2 | async-start | bytes 65536 | tf_op jit(solution)/shard_map/all_to_all | solution.py:94
  92.6 24.8 %copy-start.6 = (f32[2,32,256]{2,1,0:T(8,128)}, f32[2,32,256]{2,1,0:T(8,128)S(1)}, u32[]{:S(2)}) copy-start(f32[2,32,256]{2,1,0:T(8,128)S(1)} %convolution_select_fusion.2) | copy-start | bytes 196612
  100.7 16.2 %copy-start.2 = (bf16[2,8,16,128,32]{3,4,1,2,0:T(8,128)(2,1)S(1)}, bf16[2,8,16,128,32]{3,4,1,2,0:T(8,128)(2,1)}, u32[]{:S(2)}) copy-start(bf16[2,8,16,128,32]{3,4,1,2,0:T(8,128)(2,1)} %copy-done.1) | copy-start | bytes 6291460
  117.9 10.0 %copy-start.10 = (s32[1,128]{1,0:T(1,128)S(1)}, s32[1,128]{1,0:T(1,128)}, u32[]{:S(2)}) copy-start(s32[1,128]{1,0:T(1,128)} %param.11) | copy-start | bytes 1540
  119.5 8.3 %all-to-all-start.3 = ((bf16[2,16,8,1,128]{4,1,3,0,2:T(8,128)(2,1)}), bf16[2,16,8,1,128]{4,1,3,0,2:T(8,128)(2,1)S(1)}, u32[]{:S(2)}, u32[]{:S(2)}) async-start(bf16[2,16,8,1,128]{4,1,3,0,2:T(8,128)(2,1)} %copy.76), calls=%async_computation.4 | async-start | bytes 131072 | tf_op jit(solution)/shard_map/all_to_all | solution.py:94
  122.9 39.6 %reduce-scatter.5.cloned.1.call-start = ((), (), s32[]{:S(2)}) async-start(), calls=%async_computation.9 | async-start | bytes 655360 | tf_op jit(solution)/shard_map/reduce_scatter | solution.py:84
  127.8 10.9 %copy-start.3 = (bf16[2,8,16,128,32]{3,4,1,2,0:T(8,128)(2,1)S(1)}, bf16[2,8,16,128,32]{3,4,1,2,0:T(8,128)(2,1)}, u32[]{:S(2)}) copy-start(bf16[2,8,16,128,32]{3,4,1,2,0:T(8,128)(2,1)} %copy-done.1) | copy-start | bytes 6291460
  128.1 13.5 %copy-start.5 = (f32[1,128,256]{2,1,0:T(8,128)}, f32[1,128,256]{2,1,0:T(8,128)S(1)}, u32[]{:S(2)}) copy-start(f32[1,128,256]{2,1,0:T(8,128)S(1)} %fusion.10) | copy-start | bytes 393220
Sparse Core Ops, SparseCore 0:
  60.2 21.5 reduce-scatter.2
  144.3 18.1 reduce-scatter.4
where the time goes:
time: 181 us; the launch traced here: 180 us
  waiting for transfers between devices  74.6 us (41%)
  blocking collectives  39 us (22%)
  matrix products  21.5 us (12%)
  between operations  14.5 us (8%)
  starting transfers between devices  12.6 us (7%)
  local copies, waits for them, and re-layouts  12.5 us (7%)
  other arithmetic  5.39 us (3%)
    reduce_scatter x2, waiting for transfers between devices, forward_sum(): lax.psum_scatter(partial_value.astype(jnp.bfloat16), 'rcv', scatter_dimen...  39.5 us
    all_to_all x1, waiting for transfers between devices, body(): lax.all_to_all(reflection, 'shot', split_axis=1, concat_axis=3, tiled=True)  25.4 us
    all_gather x1, blocking collectives, focal_rows(): return lax.all_gather(pieces, 'rcv', axis=3, tiled=True)  16.1 us
    all_to_all x2, blocking collectives, spectrum_layout(): lax.all_to_all(spectra, 'shot', split_axis=1, concat_axis=2, tiled=True)  14.6 us
    dot_general x8, matrix products, product_term(): jnp.einsum('fdau,fpd->fapu', left_op, right_op, preferred_element_type=jn...  12.9 us
    all_to_all x2, waiting for transfers between devices, time_layout(): lax.all_to_all(spectra.astype(jnp.bfloat16), 'shot', split_axis=2, concat...  9.71 us
    all_to_all x1, blocking collectives, time_layout(): lax.all_to_all(spectra.astype(jnp.bfloat16), 'shot', split_axis=2, concat...  8.29 us
    all_to_all x2, starting transfers between devices, time_layout(): lax.all_to_all(spectra.astype(jnp.bfloat16), 'shot', split_axis=2, concat...  6.99 us
  transfers between devices with their start and end apart: 5, of which 5 were waited for; matrix products, arithmetic and copies ran while one was open for 1% of the time, Pallas kernels for 0%

commit v1 on v0

--- a/solution.py
+++ b/solution.py
@@ -127,7 +127,12 @@
     reflection = (complex_product(complex_product(raw_spec, delays), wavelet) * gain_factor).astype(
         jnp.bfloat16
     )
-    owned = lax.all_to_all(reflection, "shot", split_axis=1, concat_axis=3, tiled=True)
+    owned = jnp.concatenate(
+        lax.all_to_all(
+            jnp.stack(jnp.split(reflection, lax.axis_size("shot"), axis=1)), "shot", 0, 0
+        ),
+        axis=3,
+    )
     matrix = owned.reshape(2, per_owner, receiver_local, shot_count, source_local)
     upper_band = lax.dynamic_slice_in_dim(
         upper_part.reshape(NT, 2, NF), shot_index * per_owner, per_owner, 2

time: 181 us -> 202 us (1.12)
  local copies, waits for them, and re-layouts: 12.5 us -> 27.7 us
  matrix products: 21.5 us -> 25.3 us
    unnamed x28 -> x37, local copies, waits for them, and re-layouts: 2.55 us -> 13.8 us
    convert_element_type x2, local copies, waits for them, and re-layouts: 0.15 us -> 2.94 us  [body(): echo_spec = to_spectrum(upgoing_first, forward).astype(jnp.bfloat16)]
    convert_element_type x1 -> x0, local copies, waits for them, and re-layouts: 2.66 us -> none  [body(): (complex_product(complex_product(raw_spec, delays), wavelet) * gain_facto...]
    all_to_all x1 -> x0, local copies, waits for them, and re-layouts: 2.21 us -> none  [body(): lax.all_to_all(reflection, 'shot', split_axis=1, concat_axis=3, tiled=True)]
  transfers between devices with their start and end apart: 5 -> 5, of which waited for: 5 -> 5; matrix products, arithmetic and copies ran while one was open for 1% -> 2% of each run, Pallas kernels for 0% -> 0%
where the time goes in v1:
time: 202 us; the launch traced here: 201 us
  waiting for transfers between devices  73.3 us (36%)
  blocking collectives  40.4 us (20%)
  local copies, waits for them, and re-layouts  27.7 us (14%)
  matrix products  25.3 us (13%)
  between operations  14.4 us (7%)
  starting transfers between devices  13.5 us (7%)
  other arithmetic  6.73 us (3%)
    reduce_scatter x2, waiting for transfers between devices, forward_sum(): lax.psum_scatter(partial_value.astype(jnp.bfloat16), 'rcv', scatter_dimen...  38.8 us
    all_to_all x1, waiting for transfers between devices, body(): lax.all_to_all(jnp.stack(jnp.split(reflection, lax.axis_size('shot'), axi...  25.4 us
    all_to_all x2, blocking collectives, spectrum_layout(): lax.all_to_all(spectra, 'shot', split_axis=1, concat_axis=2, tiled=True)  16.2 us
    all_gather x1, blocking collectives, focal_rows(): return lax.all_gather(pieces, 'rcv', axis=3, tiled=True)  15.9 us
    unnamed x37, local copies, waits for them, and re-layouts  13.8 us
    dot_general x8, matrix products, product_term(): jnp.einsum('fdau,fpd->fapu', left_op, right_op, preferred_element_type=jn...  13 us
    all_to_all x2, waiting for transfers between devices, time_layout(): lax.all_to_all(spectra.astype(jnp.bfloat16), 'shot', split_axis=2, concat...  9.1 us
    all_to_all x1, blocking collectives, time_layout(): lax.all_to_all(spectra.astype(jnp.bfloat16), 'shot', split_axis=2, concat...  8.26 us
  transfers between devices with their start and end apart: 5, of which 5 were waited for; matrix products, arithmetic and copies ran while one was open for 2% of the time, Pallas kernels for 0%

profile of v1, /device:TPU:0, one launch (start us, length us, event | category | flops | bytes accessed | tf_op | source)
XLA Modules:
  0.0 201.3 jit_solution(16214297581110870226)
XLA Ops:
  10.9 1.8 convolution_bitcast_fusion
  12.7 1.5 subtract_bitcast_fusion
  14.3 1.3 add_bitcast_fusion.1
  22.1 5.3 %all-to-all-start = ((bf16[8,2,16,128,32]{3,2,4,1,0:T(8,128)(2,1)}), bf16[8,2,16,128,32]{3,2,4,1,0:T(8,128)(2,1)}, u32[]{:S(2)}, u32[]{:S(2)}) async-start(bf16[8,2,16,128,32]{3,2,4,1,0:T(8,128)(2,1)} %fusion.37), calls=%async_computation | async-start | bytes 4194304 | tf_op jit(solution)/shard_map/all_to_all | solution.py:131
  28.8 25.4 %all-to-all-done = bf16[8,2,16,128,32]{3,2,4,1,0:T(8,128)(2,1)} async-done(((bf16[8,2,16,128,32]{3,2,4,1,0:T(8,128)(2,1)}), bf16[8,2,16,128,32]{3,2,4,1,0:T(8,128)(2,1)}, u32[]{:S(2)}, u32[]{:S(2)}) %all-to-all-start) | async-done | bytes 2097184 | tf_op jit(solution)/shard_map/all_to_all | solution.py:131
  54.2 1.9 slice_bitcast_fusion
  56.1 1.5 fusion.34
  57.6 1.5 fusion.32
  59.0 1.5 fusion.8
  60.5 1.5 fusion.7
  64.3 20.5 %reduce-scatter.3.cloned.1.call-done = bf16[2,16,8,2,32]{4,2,1,0,3:T(8,128)(2,1)} async-done(((bf16[2,16,8,8,32]{4,2,1,0,3:T(8,128)(2,1)}), bf16[2,16,8,2,32]{4,2,1,0,3:T(8,128)(2,1)}) %reduce-scatter.3.cloned.1.call-update) | async-done | bytes 32784 | tf_op jit(solution)/shard_map/reduce_scatter | solution.py:84
  84.8 1.7 copy.201
  86.5 1.7 reshape.232
  88.2 4.0 %all-to-all-start.1 = ((bf16[8,2,1024]{2,1,0:T(2,128)(2,1)}), bf16[8,2,1024]{2,1,0:T(2,128)(2,1)}, u32[]{:S(2)}, u32[]{:S(2)}) async-start(bf16[8,2,1024]{2,1,0:T(2,128)(2,1)} %reshape.232), calls=%async_computation.2 | async-start | bytes 65536 | tf_op jit(solution)/shard_map/all_to_all | solution.py:94
  92.1 4.8 %all-to-all-done.1 = bf16[8,2,1024]{2,1,0:T(2,128)(2,1)} async-done(((bf16[8,2,1024]{2,1,0:T(2,128)(2,1)}), bf16[8,2,1024]{2,1,0:T(2,128)(2,1)}, u32[]{:S(2)}, u32[]{:S(2)}) %all-to-all-start.1) | async-done | bytes 32800 | tf_op jit(solution)/shard_map/all_to_all | solution.py:94
  97.0 1.6 reshape.233
  102.4 1.4 convert_element_type.103
  103.8 1.6 copy.105
  105.3 1.7 reshape.234
  107.0 8.8 %all_to_all.83 = bf16[8,2,1024]{2,1,0:T(2,128)(2,1)} all-to-all(bf16[8,2,1024]{2,1,0:T(2,128)(2,1)} %reshape.234), channel_id=1, replica_groups=mesh['shot'=8,'rcv'=4] {'shot'}, dimensions={0} | all-to-all | bytes 65536 | tf_op jit(solution)/shard_map/all_to_all | solution.py:100
  115.8 1.6 reshape.235
  118.3 15.9 %all-gather = bf16[2,16,8,1,8,32]{5,2,3,1,0,4:T(8,128)(2,1)S(1)} all-gather(bf16[2,16,8,1,2,32]{5,2,3,1,0,4:T(8,128)(2,1)S(1)} %copy.107), channel_id=2, replica_groups=mesh['shot'=8,'rcv'=4] {'rcv'}, dimensions={4}, use_global_device_ids=true | all-gather | bytes 163840 | tf_op jit(solution)/shard_map/all_gather | solution.py:90
  137.3 4.0 %all-to-all-start.3 = ((bf16[2,16,8,1,128]{4,1,3,0,2:T(8,128)(2,1)}), bf16[2,16,8,1,128]{4,1,3,0,2:T(8,128)(2,1)}, u32[]{:S(2)}, u32[]{:S(2)}) async-start(bf16[2,16,8,1,128]{4,1,3,0,2:T(8,128)(2,1)} %copy.114), calls=%async_computation.4 | async-start | bytes 131072 | tf_op jit(solution)/shard_map/all_to_all | solution.py:94
  142.0 4.3 %all-to-all-done.3 = bf16[2,16,8,1,128]{4,1,3,0,2:T(8,128)(2,1)} async-done(((bf16[2,16,8,1,128]{4,1,3,0,2:T(8,128)(2,1)}), bf16[2,16,8,1,128]{4,1,3,0,2:T(8,128)(2,1)}, u32[]{:S(2)}, u32[]{:S(2)}) %all-to-all-start.3) | async-done | bytes 65568 | tf_op jit(solution)/shard_map/all_to_all | solution.py:94
  148.4 1.4 fusion.14
  149.9 7.4 %all_to_all.84 = bf16[2,128,1,1,128]{4,0,3,2,1:T(2,128)(2,1)S(1)} all-to-all(bf16[2,128,1,1,128]{4,0,3,2,1:T(2,128)(2,1)S(1)} %copy.116), channel_id=1, replica_groups=mesh['shot'=8,'rcv'=4] {'shot'}, dimensions={1} | all-to-all | bytes 131072 | tf_op jit(solution)/shard_map/all_to_all | solution.py:100
  157.3 2.7 %fusion.28 = f32[16,8,8,32]{3,1,2,0:T(8,128)S(1)} fusion(bf16[16,128,8,32]{1,0,3,2:T(8,128)(2,1)} %copy-done.1, bf16[2,16,8,1,1,128]{5,2,1,4,3,0:T(8,128)(2,1)S(1)} %bitcast.206), kind=kOutput, calls=%fused_computation.55 | convolution fusion | flops 8388608 | bytes 1212416 | tf_op jit(solution)/shard_map/fdau,fpd->fapu/dot_general | solution.py:50
  160.0 1.5 fusion.26
  161.5 1.5 fusion.6
  163.0 1.5 fusion.5
  165.5 18.3 %reduce-scatter.5.cloned.1.call-done = bf16[2,16,8,2,32]{4,2,1,0,3:T(8,128)(2,1)} async-done(((bf16[2,16,8,8,32]{4,2,1,0,3:T(8,128)(2,1)}), bf16[2,16,8,2,32]{4,2,1,0,3:T(8,128)(2,1)}) %reduce-scatter.5.cloned.1.call-update) | async-done | bytes 32784 | tf_op jit(solution)/shard_map/reduce_scatter | solution.py:84
  185.0 8.3 %all_to_all.85 = bf16[8,2,1024]{2,1,0:T(2,128)(2,1)S(1)} all-to-all(bf16[8,2,1024]{2,1,0:T(2,128)(2,1)S(1)} %reshape.236), channel_id=1, replica_groups=mesh['shot'=8,'rcv'=4] {'shot'}, dimensions={0} | all-to-all | bytes 65536 | tf_op jit(solution)/shard_map/all_to_all | solution.py:94
  (83 shorter events, 28.0 us)
Async XLA Ops:
  7.2 1.6 copy-start
  9.5 0.8 copy-start.9
  9.5 1.4 copy-start.8
  22.1 6.2 %copy-start.4 = (bf16[8,128,256]{2,1,0:T(8,128)(2,1)S(1)}, bf16[8,128,256]{2,1,0:T(8,128)(2,1)}, u32[]{:S(2)}) copy-start(bf16[8,128,256]{2,1,0:T(8,128)(2,1)} %param.9) | copy-start | bytes 1572868
  22.1 32.1 %all-to-all-start = ((bf16[8,2,16,128,32]{3,2,4,1,0:T(8,128)(2,1)}), bf16[8,2,16,128,32]{3,2,4,1,0:T(8,128)(2,1)}, u32[]{:S(2)}, u32[]{:S(2)}) async-start(bf16[8,2,16,128,32]{3,2,4,1,0:T(8,128)(2,1)} %fusion.37), calls=%async_computation | async-start | bytes 4194304 | tf_op jit(solution)/shard_map/all_to_all | solution.py:131
  27.4 57.4 %reduce-scatter.3.cloned.1.call-start = ((), (), s32[]{:S(2)}) async-start(), calls=%async_computation.8 | async-start | bytes 655360 | tf_op jit(solution)/shard_map/reduce_scatter | solution.py:84
  56.1 4.4 %copy-start.1 = (bf16[16,128,8,32]{1,0,3,2:T(8,128)(2,1)}, bf16[16,128,8,32]{1,0,3,2:T(8,128)(2,1)S(1)}, u32[]{:S(2)}) copy-start(bf16[16,128,8,32]{1,0,3,2:T(8,128)(2,1)S(1)} %get-tuple-element.7) | copy-start | bytes 3145732
  62.0 37.6 %copy-start.10 = (s32[2,32]{1,0:T(2,128)S(1)}, s32[2,32]{1,0:T(2,128)}, u32[]{:S(2)}) copy-start(s32[2,32]{1,0:T(2,128)} %param.10) | copy-start | bytes 772
  88.2 8.8 %all-to-all-start.1 = ((bf16[8,2,1024]{2,1,0:T(2,128)(2,1)}), bf16[8,2,1024]{2,1,0:T(2,128)(2,1)}, u32[]{:S(2)}, u32[]{:S(2)}) async-start(bf16[8,2,1024]{2,1,0:T(2,128)(2,1)} %reshape.232), calls=%async_computation.2 | async-start | bytes 65536 | tf_op jit(solution)/shard_map/all_to_all | solution.py:94
  100.8 0.6 copy-start.7
  134.3 1.2 copy-start.2
  135.5 11.7 %copy-start.11 = (s32[1,128]{1,0:T(1,128)S(1)}, s32[1,128]{1,0:T(1,128)}, u32[]{:S(2)}) copy-start(s32[1,128]{1,0:T(1,128)} %param.11) | copy-start | bytes 1540
  137.3 9.0 %all-to-all-start.3 = ((bf16[2,16,8,1,128]{4,1,3,0,2:T(8,128)(2,1)}), bf16[2,16,8,1,128]{4,1,3,0,2:T(8,128)(2,1)}, u32[]{:S(2)}, u32[]{:S(2)}) async-start(bf16[2,16,8,1,128]{4,1,3,0,2:T(8,128)(2,1)} %copy.114), calls=%async_computation.4 | async-start | bytes 131072 | tf_op jit(solution)/shard_map/all_to_all | solution.py:94
  141.3 42.6 %reduce-scatter.5.cloned.1.call-start = ((), (), s32[]{:S(2)}) async-start(), calls=%async_computation.9 | async-start | bytes 655360 | tf_op jit(solution)/shard_map/reduce_scatter | solution.py:84
  146.3 13.7 %copy-start.3 = (bf16[16,128,8,32]{1,0,3,2:T(8,128)(2,1)S(1)}, bf16[16,128,8,32]{1,0,3,2:T(8,128)(2,1)}, u32[]{:S(2)}) copy-start(bf16[16,128,8,32]{1,0,3,2:T(8,128)(2,1)} %copy-done.1) | copy-start | bytes 3145732
  148.4 8.9 %copy-start.6 = (f32[1,128,256]{2,1,0:T(8,128)}, f32[1,128,256]{2,1,0:T(8,128)S(1)}, u32[]{:S(2)}) copy-start(f32[1,128,256]{2,1,0:T(8,128)S(1)} %fusion.10) | copy-start | bytes 393220
  164.4 29.1 %copy-start.5 = (f32[256,128]{0,1:T(8,128)S(1)}, f32[256,128]{0,1:T(8,128)}, u32[]{:S(2)}) copy-start(f32[256,128]{0,1:T(8,128)} %get-tuple-element.15) | copy-start | bytes 393220
Sparse Core Ops, SparseCore 0:
  63.2 21.5 reduce-scatter.2
  165.6 18.1 reduce-scatter.4
